TPU v7x, 256 devices: a whole 4x4x8 slice. The times are simulated.
256 devices in a mesh: row: 16 (over z, core), col: 16 (over x, y).
Axes of the slice: x: 4, y: 4, z: 8, core: 2. Of those that a mesh axis runs over, the one named last changes fastest.
Arguments:
- tensor: float32 [12, 8192, 8192], P(None, 'row', 'col'), may hold values from -6 to 6
- factor_b: float32 [8192, 128], P(('col', 'row')), may hold values from -0.0625 to 0.0625
- factor_c: float32 [12, 128], replicated, may hold values from -1.75 to 1.75
Outputs:
- a_update: float32 [8192, 128], P(('row', 'col'))
- b_update: float32 [8192, 128], P(('col', 'row'))
All inputs are finite; a program needn't handle non-finite values.
Results may differ from a plain program's by a relative error of at most 0.00012.
Values sent between devices are 32-bit elements; how exact they have to be, the bound alone decides.
No kernel may reach another device: no remote copies, remote signals or barrier semaphores. Data moves between devices by JAX's collectives and lax.ppermute only.
A program may use at most 64 MiB of HBM per device.

v0:
```python
import jax
import jax.numpy as jnp
from jax import lax
from jax.sharding import PartitionSpec as P

EPSILON = 1e-06


def solve_system(rhs, system):
    highest = lax.Precision.HIGHEST
    lower = jnp.linalg.cholesky(system)
    inverse = jax.scipy.linalg.cho_solve(
        (lower, True), jnp.eye(system.shape[0], dtype=system.dtype)
    )
    return jnp.dot(rhs, inverse, precision=highest)


def gram_of(matrix):
    return jnp.dot(matrix.T, matrix, precision=lax.Precision.HIGHEST)


def per_device(tensor, factor_b, factor_c):
    highest = lax.Precision.HIGHEST
    rows_block = tensor.shape[1]
    cols_block = tensor.shape[2]
    rank_width = factor_c.shape[1]
    owned_a = rows_block // lax.axis_size("col")
    owned_b = cols_block // lax.axis_size("row")
    c_gram = gram_of(factor_c)
    empty_b = jnp.zeros((cols_block, rank_width), jnp.float32)
    gram_b = lax.psum(gram_of(factor_b), ("row", "col"))
    block = tensor
    khatri = factor_c[:, None, :] * lax.all_gather(factor_b, "row", axis=0, tiled=True)[None, :, :]
    partial_a = jnp.einsum("kij,kjr->ir", block, khatri, precision=highest)
    whole_a = lax.psum(partial_a, "col")
    summed_a = lax.dynamic_slice_in_dim(whole_a, lax.axis_index("col") * owned_a, owned_a, 0)
    a_update = solve_system(summed_a, c_gram * gram_b)
    squares = lax.psum(jnp.sum(a_update * a_update, axis=0), ("row", "col"))
    factor_a = a_update / jnp.sqrt(squares + EPSILON)
    gram_a = lax.psum(gram_of(factor_a), ("row", "col"))
    block = tensor
    khatri = factor_c[:, None, :] * lax.all_gather(factor_a, "col", axis=0, tiled=True)[None, :, :]
    partial_b = empty_b + jnp.einsum("kij,kir->jr", block, khatri, precision=highest)
    whole_b = lax.psum(partial_b, "row")
    summed_b = lax.dynamic_slice_in_dim(whole_b, lax.axis_index("row") * owned_b, owned_b, 0)
    b_update = solve_system(summed_b, c_gram * gram_a)
    return (a_update, b_update)


def solution(mesh):
    placed = (P(None, "row", "col"), P(("col", "row"), None), P())
    return jax.shard_map(
        per_device,
        mesh=mesh,
        in_specs=placed,
        out_specs=(P(("row", "col"), None), P(("col", "row"), None)),
        check_vma=False,
    )
```

profile of v0, /device:TPU:1, one launch (start us, length us, event | category | flops | bytes accessed | tf_op | source)
XLA Modules:
  0.0 809.7 jit_solution(5450451104905007428)
XLA Ops:
  7.2 1.7 fusion.35
  8.9 0.0 all-reduce.5.cloned.1.call-start
  9.0 22.3 %all_gather.6 = f32[512,128]{1,0:T(8,128)S(1)} all-gather(f32[32,128]{1,0:T(8,128)} %param.7), channel_id=1, replica_groups=mesh['row'=16,'col'=16] {'row'}, dimensions={0}, use_global_device_ids=true | all-gather | bytes 278528 | tf_op jit(solution)/shard_map/all_gather | solution.py:33
  31.2 18.3 %fusion.8 = f32[512,128]{0,1:T(8,128)} fusion(f32[12,512,512]{2,1,0:T(8,128)} %param.6, f32[512,128]{1,0:T(8,128)S(1)} %all_gather.6, f32[12,128]{1,0:T(8,128)} %param.8), kind=kOutput, calls=%fused_computation.8 | convolution fusion | flops 4832624640 | bytes 13113344 | tf_op jit(solution)/shard_map/kij,kjr->ir/dot_general | solution.py:34
  49.6 0.2 all-reduce.11.cloned.1.call-start
  49.8 209.2 %all-reduce.7.cloned.1.call-done = f32[128,128]{0,1:T(8,128)} async-done(((f32[128,128]{0,1:T(8,128)}), f32[128,128]{0,1:T(8,128)}) %all-reduce.7.cloned.1.call-update) | async-done | bytes 65552 | tf_op jit(solution)/shard_map/psum | solution.py:31
  259.1 1.1 fusion.34
  260.2 0.1 copy.7
  260.3 11.7 %cholesky.44 = f32[128,128]{1,0:T(8,128)S(1)} custom-call(f32[128,128]{1,0:T(8,128)S(1)} %fusion.27), custom_call_target="Cholesky" | custom-call | tf_op jit(solution)/shard_map/jit(cholesky)/cholesky | solution.py:11
  272.1 0.6 compare_reduce_fusion.1
  272.7 0.7 fusion.18
  273.4 9.8 %custom-call.8 = f32[1,128,128]{1,2,0:T(8,128)S(1)} custom-call(f32[1,128,128]{2,1,0:T(8,128)S(1)} %fusion.18), custom_call_target="InvertDiagBlocksLowerTriangular" | custom-call | tf_op jit(solution)/shard_map/jit(_cho_solve)/triangular_solve | solution.py:12
  283.2 0.3 fusion.16
  283.5 0.2 fusion.24
  283.7 68.0 %all-reduce.5.cloned.1.call-done = f32[512,128]{0,1:T(8,128)} async-done(((f32[512,128]{0,1:T(8,128)}), f32[512,128]{0,1:T(8,128)}) %all-reduce.5.cloned.1.call-update) | async-done | bytes 262160 | tf_op jit(solution)/shard_map/psum | solution.py:35
  351.7 1.2 multiply_reduce_fusion
  352.8 77.5 %psum.37 = f32[128]{0:T(128)S(1)} all-reduce(f32[128]{0:T(128)S(1)} %get-tuple-element.6), channel_id=1, replica_groups=mesh['row'=16,'col'=16] {'row','col'}, use_global_device_ids=true, to_apply=%region_5.0 | all-reduce | flops 128 | bytes 1024 | tf_op jit(solution)/shard_map/psum | solution.py:38
  430.3 0.9 fusion.36
  431.3 15.8 %all_gather.7 = f32[512,128]{1,0:T(8,128)S(1)} all-gather(f32[32,128]{1,0:T(8,128)S(1)} %broadcast_divide_fusion), channel_id=1, replica_groups=mesh['row'=16,'col'=16] {'col'}, dimensions={0}, use_global_device_ids=true | all-gather | bytes 278528 | tf_op jit(solution)/shard_map/all_gather | solution.py:42
  447.1 0.3 all-reduce.9.cloned.1.call-start
  447.3 11.4 %fusion.11 = f32[512,128]{0,1:T(8,128)} fusion(f32[12,512,512]{2,1,0:T(8,128)} %param.6, f32[512,128]{1,0:T(8,128)S(1)} %all_gather.7, f32[12,128]{1,0:T(8,128)S(1)} %copy-done), kind=kOutput, calls=%fused_computation.9 | convolution fusion | flops 4832624640 | bytes 13113344 | tf_op jit(solution)/shard_map/kij,kir->jr/dot_general | solution.py:43
  458.8 234.0 %all-reduce.11.cloned.1.call-done = f32[128,128]{0,1:T(8,128)} async-done(((f32[128,128]{0,1:T(8,128)}), f32[128,128]{0,1:T(8,128)}) %all-reduce.11.cloned.1.call-update) | async-done | bytes 65552 | tf_op jit(solution)/shard_map/psum | solution.py:40
  692.8 0.9 mul.48
  693.7 0.1 copy.10
  693.8 11.7 %cholesky.55 = f32[128,128]{1,0:T(8,128)S(1)} custom-call(f32[128,128]{1,0:T(8,128)S(1)} %fusion.23), custom_call_target="Cholesky" | custom-call | tf_op jit(solution)/shard_map/jit(cholesky)/cholesky | solution.py:11
  705.5 0.6 compare_reduce_fusion
  706.2 0.7 fusion.19
  706.8 9.8 %custom-call.9 = f32[1,128,128]{1,2,0:T(8,128)S(1)} custom-call(f32[1,128,128]{2,1,0:T(8,128)S(1)} %fusion.19), custom_call_target="InvertDiagBlocksLowerTriangular" | custom-call | tf_op jit(solution)/shard_map/jit(_cho_solve)/triangular_solve | solution.py:12
  716.7 0.3 fusion.14
  716.9 0.2 fusion.20
  717.2 84.3 %all-reduce.9.cloned.1.call-done = f32[512,128]{0,1:T(8,128)} async-done(((f32[512,128]{0,1:T(8,128)}), f32[512,128]{0,1:T(8,128)}) %all-reduce.9.cloned.1.call-update) | async-done | bytes 262160 | tf_op jit(solution)/shard_map/psum | solution.py:44
  801.4 1.8 fusion.28
  (15 shorter events, 0.2 us)
Async XLA Ops:
  7.2 251.9 %all-reduce.7.cloned.1.call-start = ((), (), s32[]{:S(2)}) async-start(), calls=%async_computation.1 | async-start | bytes 131072 | tf_op jit(solution)/shard_map/psum | solution.py:31
  8.9 342.7 %all-reduce.5.cloned.1.call-start = ((), (), s32[]{:S(2)}) async-start(), calls=%async_computation | async-start | bytes 524288 | tf_op jit(solution)/shard_map/psum | solution.py:35
  31.2 227.8 %copy-start = (f32[12,128]{1,0:T(8,128)S(1)}, f32[12,128]{1,0:T(8,128)}, u32[]{:S(2)}) copy-start(f32[12,128]{1,0:T(8,128)} %param.8) | copy-start | bytes 18436
  49.6 643.2 %all-reduce.11.cloned.1.call-start = ((), (), s32[]{:S(2)}) async-start(), calls=%async_computation.3 | async-start | bytes 131072 | tf_op jit(solution)/shard_map/psum | solution.py:40
  352.8 105.9 %copy-start.1 = (f32[32,128]{1,0:T(8,128)}, f32[32,128]{1,0:T(8,128)S(1)}, u32[]{:S(2)}) copy-start(f32[32,128]{1,0:T(8,128)S(1)} %get-tuple-element.7) | copy-start | bytes 49156
  447.1 354.4 %all-reduce.9.cloned.1.call-start = ((), (), s32[]{:S(2)}) async-start(), calls=%async_computation.2 | async-start | bytes 524288 | tf_op jit(solution)/shard_map/psum | solution.py:44
Sparse Core Ops, SparseCore 0:
  13.5 245.5 all-reduce.6
  262.2 89.3 all-reduce.4
  447.2 245.5 all-reduce.10
  695.0 106.4 all-reduce.8
where the time goes:
time: 810 us
  waiting for transfers between devices  596 us (74%)
  blocking collectives  116 us (14%)
  other arithmetic  46.6 us (6%)
  matrix products  37.4 us (5%)
  between operations  13.9 us (2%)
    psum x1, waiting for transfers between devices, per_device(): gram_a = lax.psum(gram_of(factor_a), ('row', 'col'))  234 us
    psum x1, waiting for transfers between devices, per_device(): gram_b = lax.psum(gram_of(factor_b), ('row', 'col'))  209 us
    psum x1, waiting for transfers between devices, per_device(): whole_b = lax.psum(partial_b, 'row')  84.3 us
    psum x1, blocking collectives, per_device(): squares = lax.psum(jnp.sum(a_update * a_update, axis=0), ('row', 'col'))  77.5 us
    psum x1, waiting for transfers between devices, per_device(): whole_a = lax.psum(partial_a, 'col')  68 us
    another operation x6, other arithmetic, solve_system(): lower = jnp.linalg.cholesky(system)  24.8 us
    all_gather x1, blocking collectives, per_device(): lax.all_gather(factor_b, 'row', axis=0, tiled=True)[None, :, :]  22.3 us
    another operation x4, other arithmetic, solve_system(): jax.scipy.linalg.cho_solve((lower, True), jnp.eye(system.shape[0], dtype=...  20.9 us
  transfers between devices with their start and end apart: 4, of which 4 were waited for; matrix products, arithmetic and copies ran while one was open for 10% of the time, Pallas kernels for 0%

commit v1 on v0

--- a/solution.py
+++ b/solution.py
@@ -37,7 +37,7 @@
     a_update = solve_system(summed_a, c_gram * gram_b)
     squares = lax.psum(jnp.sum(a_update * a_update, axis=0), ("row", "col"))
     factor_a = a_update / jnp.sqrt(squares + EPSILON)
-    gram_a = lax.psum(gram_of(factor_a), ("row", "col"))
+    gram_a = lax.psum(lax.psum(gram_of(factor_a), "col"), "row")
     block = tensor
     khatri = factor_c[:, None, :] * lax.all_gather(factor_a, "col", axis=0, tiled=True)[None, :, :]
     partial_b = empty_b + jnp.einsum("kij,kir->jr", block, khatri, precision=highest)

time: 810 us -> 686 us (0.85)
  waiting for transfers between devices: 596 us -> 472 us
    psum x2, waiting for transfers between devices: 318 us -> 194 us  [per_device(): gram_a = lax.psum(lax.psum(gram_of(factor_a), 'col'), 'row')]
  transfers between devices with their start and end apart: 4 -> 4, of which waited for: 4 -> 4; matrix products, arithmetic and copies ran while one was open for 10% -> 8% of each run, Pallas kernels for 0% -> 0%
where the time goes in v1:
time: 686 us
  waiting for transfers between devices  472 us (69%)
  blocking collectives  116 us (17%)
  other arithmetic  46.6 us (7%)
  matrix products  37.5 us (5%)
  between operations  13.9 us (2%)
    psum x1, waiting for transfers between devices, per_device(): gram_b = lax.psum(gram_of(factor_b), ('row', 'col'))  209 us
    psum x2, waiting for transfers between devices, per_device(): gram_a = lax.psum(lax.psum(gram_of(factor_a), 'col'), 'row')  194 us
    psum x1, blocking collectives, per_device(): squares = lax.psum(jnp.sum(a_update * a_update, axis=0), ('row', 'col'))  77.5 us
    psum x1, waiting for transfers between devices, per_device(): whole_a = lax.psum(partial_a, 'col')  68 us
    another operation x6, other arithmetic, solve_system(): lower = jnp.linalg.cholesky(system)  24.8 us
    all_gather x1, blocking collectives, per_device(): lax.all_gather(factor_b, 'row', axis=0, tiled=True)[None, :, :]  22.3 us
    another operation x4, other arithmetic, solve_system(): jax.scipy.linalg.cho_solve((lower, True), jnp.eye(system.shape[0], dtype=...  20.9 us
    dot_general x1, matrix products, per_device(): partial_a = jnp.einsum('kij,kjr->ir', block, khatri, precision=highest)  18.3 us
  transfers between devices with their start and end apart: 4, of which 4 were waited for; matrix products, arithmetic and copies ran while one was open for 8% of the time, Pallas kernels for 0%

profile of v1, /device:TPU:1, one launch (start us, length us, event | category | flops | bytes accessed | tf_op | source)
XLA Modules:
  0.0 685.9 jit_solution(141782250365787634)
XLA Ops:
  7.2 1.7 fusion.35
  8.9 0.0 all-reduce.6.cloned.1.call-start
  9.0 22.3 %all_gather.6 = f32[512,128]{1,0:T(8,128)S(1)} all-gather(f32[32,128]{1,0:T(8,128)} %param.7), channel_id=1, replica_groups=mesh['row'=16,'col'=16] {'row'}, dimensions={0}, use_global_device_ids=true | all-gather | bytes 278528 | tf_op jit(solution)/shard_map/all_gather | solution.py:33
  31.2 18.3 %fusion.8 = f32[512,128]{0,1:T(8,128)} fusion(f32[12,512,512]{2,1,0:T(8,128)} %param.6, f32[512,128]{1,0:T(8,128)S(1)} %all_gather.6, f32[12,128]{1,0:T(8,128)} %param.8), kind=kOutput, calls=%fused_computation.8 | convolution fusion | flops 4832624640 | bytes 13113344 | tf_op jit(solution)/shard_map/kij,kjr->ir/dot_general | solution.py:34
  49.6 0.2 all-reduce.10.cloned.1.call-start
  49.9 209.2 %all-reduce.8.cloned.1.call-done = f32[128,128]{0,1:T(8,128)} async-done(((f32[128,128]{0,1:T(8,128)}), f32[128,128]{0,1:T(8,128)}) %all-reduce.8.cloned.1.call-update) | async-done | bytes 65552 | tf_op jit(solution)/shard_map/psum | solution.py:31
  259.1 1.1 fusion.34
  260.2 0.1 copy.7
  260.3 11.7 %cholesky.44 = f32[128,128]{1,0:T(8,128)S(1)} custom-call(f32[128,128]{1,0:T(8,128)S(1)} %fusion.27), custom_call_target="Cholesky" | custom-call | tf_op jit(solution)/shard_map/jit(cholesky)/cholesky | solution.py:11
  272.1 0.6 compare_reduce_fusion.1
  272.7 0.7 fusion.18
  273.4 9.8 %custom-call.8 = f32[1,128,128]{1,2,0:T(8,128)S(1)} custom-call(f32[1,128,128]{2,1,0:T(8,128)S(1)} %fusion.18), custom_call_target="InvertDiagBlocksLowerTriangular" | custom-call | tf_op jit(solution)/shard_map/jit(_cho_solve)/triangular_solve | solution.py:12
  283.2 0.3 fusion.16
  283.5 0.2 fusion.24
  283.7 68.0 %all-reduce.6.cloned.1.call-done = f32[512,128]{0,1:T(8,128)} async-done(((f32[512,128]{0,1:T(8,128)}), f32[512,128]{0,1:T(8,128)}) %all-reduce.6.cloned.1.call-update) | async-done | bytes 262160 | tf_op jit(solution)/shard_map/psum | solution.py:35
  351.7 1.2 multiply_reduce_fusion
  352.8 77.5 %psum.44 = f32[128]{0:T(128)S(1)} all-reduce(f32[128]{0:T(128)S(1)} %get-tuple-element.8), channel_id=1, replica_groups=mesh['row'=16,'col'=16] {'row','col'}, use_global_device_ids=true, to_apply=%region_5.0 | all-reduce | flops 128 | bytes 1024 | tf_op jit(solution)/shard_map/psum | solution.py:38
  430.3 0.9 fusion.36
  431.2 15.8 %all_gather.7 = f32[512,128]{1,0:T(8,128)S(1)} all-gather(f32[32,128]{1,0:T(8,128)S(1)} %broadcast_divide_fusion), channel_id=1, replica_groups=mesh['row'=16,'col'=16] {'col'}, dimensions={0}, use_global_device_ids=true | all-gather | bytes 278528 | tf_op jit(solution)/shard_map/all_gather | solution.py:42
  447.1 0.3 all-reduce.12.cloned.1.call-start
  447.3 11.4 %fusion.11 = f32[512,128]{0,1:T(8,128)} fusion(f32[12,512,512]{2,1,0:T(8,128)} %param.6, f32[512,128]{1,0:T(8,128)S(1)} %all_gather.7, f32[12,128]{1,0:T(8,128)S(1)} %copy-done), kind=kOutput, calls=%fused_computation.9 | convolution fusion | flops 4832624640 | bytes 13113344 | tf_op jit(solution)/shard_map/kij,kir->jr/dot_general | solution.py:43
  458.8 82.5 %all-reduce.10.cloned.1.call-done = f32[128,128]{0,1:T(8,128)} async-done(((f32[128,128]{0,1:T(8,128)}), f32[128,128]{0,1:T(8,128)}) %all-reduce.10.cloned.1.call-update) | async-done | bytes 65552 | tf_op jit(solution)/shard_map/psum | solution.py:40
  541.4 111.9 %all-reduce.12.cloned.1.call-done = (f32[128,128]{0,1:T(8,128)}, f32[512,128]{0,1:T(8,128)}) async-done(((f32[128,128]{0,1:T(8,128)}, f32[512,128]{0,1:T(8,128)}), (f32[128,128]{0,1:T(8,128)}, f32[512,128]{0,1:T(8,128)})) %all-reduce.12.cloned.1.call-update) | async-done | bytes 327696 | tf_op jit(solution)/shard_map/psum | solution.py:40
  653.2 0.8 mul.48
  654.1 0.1 copy.10
  654.2 11.7 %cholesky.55 = f32[128,128]{1,0:T(8,128)S(1)} custom-call(f32[128,128]{1,0:T(8,128)S(1)} %fusion.23), custom_call_target="Cholesky" | custom-call | tf_op jit(solution)/shard_map/jit(cholesky)/cholesky | solution.py:11
  665.9 0.6 compare_reduce_fusion
  666.6 0.7 fusion.19
  667.2 9.8 %custom-call.9 = f32[1,128,128]{1,2,0:T(8,128)S(1)} custom-call(f32[1,128,128]{2,1,0:T(8,128)S(1)} %fusion.19), custom_call_target="InvertDiagBlocksLowerTriangular" | custom-call | tf_op jit(solution)/shard_map/jit(_cho_solve)/triangular_solve | solution.py:12
  677.1 0.3 fusion.14
  677.4 0.2 fusion.20
  677.6 1.8 fusion.28
  (15 shorter events, 0.2 us)
Async XLA Ops:
  7.2 251.9 %all-reduce.8.cloned.1.call-start = ((), (), s32[]{:S(2)}) async-start(), calls=%async_computation.1 | async-start | bytes 131072 | tf_op jit(solution)/shard_map/psum | solution.py:31
  8.9 342.7 %all-reduce.6.cloned.1.call-start = ((), (), s32[]{:S(2)}) async-start(), calls=%async_computation | async-start | bytes 524288 | tf_op jit(solution)/shard_map/psum | solution.py:35
  31.2 227.8 %copy-start = (f32[12,128]{1,0:T(8,128)S(1)}, f32[12,128]{1,0:T(8,128)}, u32[]{:S(2)}) copy-start(f32[12,128]{1,0:T(8,128)} %param.8) | copy-start | bytes 18436
  49.6 491.7 %all-reduce.10.cloned.1.call-start = ((), (), s32[]{:S(2)}) async-start(), calls=%async_computation.2 | async-start | bytes 131072 | tf_op jit(solution)/shard_map/psum | solution.py:40
  352.8 105.9 %copy-start.1 = (f32[32,128]{1,0:T(8,128)}, f32[32,128]{1,0:T(8,128)S(1)}, u32[]{:S(2)}) copy-start(f32[32,128]{1,0:T(8,128)S(1)} %get-tuple-element.9) | copy-start | bytes 49156
  447.1 206.2 %all-reduce.12.cloned.1.call-start = ((), (), s32[]{:S(2)}) async-start(), calls=%async_computation.3 | async-start | bytes 655360 | tf_op jit(solution)/shard_map/psum | solution.py:40
Sparse Core Ops, SparseCore 0:
  13.5 245.5 all-reduce.7
  262.2 89.3 all-reduce.5
  447.2 94.0 all-reduce.9
  543.6 109.5 all-reduce.11
